TPU v7x, 32 devices: a whole 2x2x4 slice. The times are simulated.
32 devices in a mesh: dp: 16 (over z, y, x), mp: 2 (over core).
Axes of the slice: x: 2, y: 2, z: 4, core: 2. Of those that a mesh axis runs over, the one named last changes fastest.
Arguments:
- hidden: bfloat16 [2, 64, 64, 768], P(None, 'dp'), may hold values from -6 to 6
- encoder_tokens: bfloat16 [2, 32, 576, 768], P(None, 'dp'), may hold values from -6 to 6
- segment_ids: int32 [2, 64, 64], P(None, 'dp'), may hold values from 0 to 3, never falling along the last dimension, each value on 1 to 32 neighbouring positions
- image_index: int32 [2, 64], P(None, 'dp'), may hold values from 0 to 1
- cotangent: bfloat16 [2, 64, 64, 768], P(None, 'dp'), may hold values from -6 to 6
- norm_gains: bfloat16 [3, 768], P(None, 'dp'), may hold values from 0.099609375 to 1.8984375
- qkv_weight: bfloat16 [3, 768, 768], P(None, 'dp', 'mp'), may hold values from -0.21875 to 0.21875
- self_out_weight: bfloat16 [768, 768], P('dp', 'mp'), may hold values from -0.875 to 0.875
- cross_query_weight: bfloat16 [768, 768], P('dp', 'mp'), may hold values from -0.21875 to 0.21875
- cross_kv_weight: bfloat16 [2, 768, 768], P(None, 'dp', 'mp'), may hold values from -0.21875 to 0.21875
- cross_out_weight: bfloat16 [768, 768], P('dp', 'mp'), may hold values from -2.5 to 2.5
- up_weight: bfloat16 [768, 3072], P('dp', 'mp'), may hold values from -0.21875 to 0.21875
- down_weight: bfloat16 [768, 3072], P('dp', 'mp'), may hold values from -0.109375 to 0.109375
Outputs:
- output: bfloat16 [2, 64, 64, 768], P(None, 'dp')
- input_grad: float32 [2, 64, 64, 768], P(None, 'dp')
- encoder_grad: float32 [2, 32, 576, 768], P(None, 'dp', None, 'mp')
- grad_norm_gains: float32 [3, 768], P(None, 'dp')
- grad_qkv: float32 [3, 768, 768], P(None, 'dp', 'mp')
- grad_self_out: float32 [768, 768], P('dp', 'mp')
- grad_cross_query: float32 [768, 768], P('dp', 'mp')
- grad_cross_kv: float32 [2, 768, 768], P(None, 'dp', 'mp')
- grad_cross_out: float32 [768, 768], P('dp', 'mp')
- grad_up: float32 [768, 3072], P('dp', 'mp')
- grad_down: float32 [768, 3072], P('dp', 'mp')
Inputs may be any that keep to these rules, and one draw needn't show every extreme that they name: `segment_ids`: within a row the ids never fall; they number the 4 captions of the row, each of 1 to 32 tokens. Caption row r of a micro-batch reads image (r // 4) * 2 + image_index of that row.
All inputs are finite; a program needn't handle non-finite values.
Results may differ from a plain program's by a relative error of at most 0.019.
Values may be sent and summed in bfloat16 or wider, within the bound.
A program may use at most 192 MiB of HBM per device.

v0:
```python
import jax
import jax.numpy as jnp
from jax import lax
from jax.sharding import PartitionSpec as P

HEAD = 64


EPSILON = 1e-05
NEGATIVE = -1e30


def layer_norm(values, gain_row):
    centred = values - jnp.mean(values, axis=-1, keepdims=True)
    spread = jnp.mean(centred * centred, axis=-1, keepdims=True)
    return centred * lax.rsqrt(spread + EPSILON) * gain_row


def gelu_exact(values):
    return jax.nn.gelu(values, approximate=False)


def token_outer(left, right):
    return lax.dot_general(
        left, right, (((0,), (0,)), ((), ())), preferred_element_type=jnp.float32
    )


def feature_inner(left, right):
    return lax.dot_general(
        left, right, (((1,), (1,)), ((), ())), preferred_element_type=jnp.float32
    )


def attend(queries, key_heads, value_heads, allowed, score_scale):
    scores = (
        jnp.einsum("rqhe,rkhe->rhqk", queries, key_heads, preferred_element_type=jnp.float32)
        * score_scale
    )
    if allowed is not None:
        scores = jnp.where(allowed[:, None], scores, NEGATIVE)
    row_max = jnp.max(scores, axis=-1, keepdims=True)
    shifted = jnp.exp(scores - row_max)
    row_total = jnp.sum(shifted, axis=-1, keepdims=True)
    weights_low = (shifted / row_total).astype(jnp.bfloat16)
    mixed_heads = jnp.einsum(
        "rhqk,rkhe->rqhe", weights_low, value_heads, preferred_element_type=jnp.float32
    )
    return (mixed_heads.astype(jnp.bfloat16), row_max + jnp.log(row_total))


def attend_back(queries, key_heads, value_heads, allowed, score_scale, log_total, grad_mixed):
    scores = (
        jnp.einsum("rqhe,rkhe->rhqk", queries, key_heads, preferred_element_type=jnp.float32)
        * score_scale
    )
    if allowed is not None:
        scores = jnp.where(allowed[:, None], scores, NEGATIVE)
    probability = jnp.exp(scores - log_total)
    grad_weights = jnp.einsum(
        "rqhe,rkhe->rhqk", grad_mixed, value_heads, preferred_element_type=jnp.float32
    )
    inner_sum = jnp.sum(probability * grad_weights, axis=-1, keepdims=True)
    grad_scores = (probability * (grad_weights - inner_sum)).astype(jnp.bfloat16)
    grad_queries = (
        jnp.einsum("rhqk,rkhe->rqhe", grad_scores, key_heads, preferred_element_type=jnp.float32)
        * score_scale
    )
    grad_keys = (
        jnp.einsum("rhqk,rqhe->rkhe", grad_scores, queries, preferred_element_type=jnp.float32)
        * score_scale
    )
    grad_values = jnp.einsum(
        "rhqk,rqhe->rkhe",
        probability.astype(jnp.bfloat16),
        grad_mixed,
        preferred_element_type=jnp.float32,
    )
    return (grad_queries, grad_keys, grad_values)


def fetch_weights(
    norm_gains,
    qkv_weight,
    self_out_weight,
    cross_query_weight,
    cross_kv_weight,
    cross_out_weight,
    up_weight,
    down_weight,
):
    return (
        lax.all_gather(norm_gains, "dp", axis=1, tiled=True),
        lax.all_gather(qkv_weight, "dp", axis=1, tiled=True),
        lax.all_gather(self_out_weight, "dp", axis=0, tiled=True),
        lax.all_gather(cross_query_weight, "dp", axis=0, tiled=True),
        lax.all_gather(cross_kv_weight, "dp", axis=1, tiled=True),
        lax.all_gather(cross_out_weight, "dp", axis=0, tiled=True),
        lax.all_gather(up_weight, "dp", axis=0, tiled=True),
        lax.all_gather(down_weight, "dp", axis=0, tiled=True),
    )


def reduce_weight_grads(gradients):
    return (
        lax.psum_scatter(gradients[0], "dp", scatter_dimension=1, tiled=True),
        lax.psum_scatter(gradients[1], "dp", scatter_dimension=1, tiled=True),
        lax.psum_scatter(gradients[2], "dp", scatter_dimension=0, tiled=True),
        lax.psum_scatter(gradients[3], "dp", scatter_dimension=0, tiled=True),
        lax.psum_scatter(gradients[4], "dp", scatter_dimension=1, tiled=True),
        lax.psum_scatter(gradients[5], "dp", scatter_dimension=0, tiled=True),
        lax.psum_scatter(gradients[6], "dp", scatter_dimension=0, tiled=True),
        lax.psum_scatter(gradients[7], "dp", scatter_dimension=0, tiled=True),
    )


def branch_output(mixed_heads, weight):
    return lax.psum(feature_inner(mixed_heads, weight), "mp")


def input_grad_sum(partial_sum):
    return lax.psum(partial_sum.astype(jnp.bfloat16), "mp").astype(jnp.float32)


def add_pair(first, second):
    return first + second


def micro_step(gathered, hidden, encoder, segment, image_ids, cotangent):
    (
        norm_gains,
        qkv_weight,
        self_out_weight,
        cross_query_weight,
        cross_kv_weight,
        cross_out_weight,
        up_weight,
        down_weight,
    ) = gathered
    row_count, length, model_width = hidden.shape
    image_count, context = (encoder.shape[0], encoder.shape[1])
    head_count = qkv_weight.shape[2] // HEAD
    tokens = row_count * length
    head_shape = (row_count, length, head_count, HEAD)
    score_scale = HEAD ** (-0.5)
    gain_rows = norm_gains.astype(jnp.float32)
    positions = jnp.arange(length)
    causal = positions[None, :] <= positions[:, None]
    allowed = causal[None] & (segment[:, :, None] == segment[:, None, :])
    flat_in = hidden.reshape(tokens, model_width).astype(jnp.float32)
    low_one = layer_norm(flat_in, gain_rows[0]).astype(jnp.bfloat16)
    projected = jnp.einsum(
        "td,jde->jte", low_one, qkv_weight, preferred_element_type=jnp.float32
    ).astype(jnp.bfloat16)
    queries = projected[0].reshape(head_shape)
    key_heads = projected[1].reshape(head_shape)
    value_heads = projected[2].reshape(head_shape)
    self_mixed, self_total = attend(queries, key_heads, value_heads, allowed, score_scale)
    self_flat = self_mixed.reshape(tokens, -1)
    resid_one = flat_in + branch_output(self_flat, self_out_weight)
    low_two = layer_norm(resid_one, gain_rows[1]).astype(jnp.bfloat16)
    cross_queries = (
        jnp.dot(low_two, cross_query_weight, preferred_element_type=jnp.float32)
        .astype(jnp.bfloat16)
        .reshape(head_shape)
    )
    image_kv = jnp.einsum(
        "ncd,jde->jnce", encoder, cross_kv_weight, preferred_element_type=jnp.float32
    ).astype(jnp.bfloat16)
    row_kv = jnp.take(image_kv, image_ids, axis=1).reshape(2, row_count, context, head_count, HEAD)
    cross_mixed, cross_total = attend(cross_queries, row_kv[0], row_kv[1], None, score_scale)
    cross_flat = cross_mixed.reshape(tokens, -1)
    resid_two = resid_one + branch_output(cross_flat, cross_out_weight)
    low_three = layer_norm(resid_two, gain_rows[2]).astype(jnp.bfloat16)
    pre_act = jnp.dot(low_three, up_weight, preferred_element_type=jnp.float32)
    activated = gelu_exact(pre_act).astype(jnp.bfloat16)
    resid_three = resid_two + branch_output(activated, down_weight)
    output_rows = resid_three.astype(jnp.bfloat16).reshape(row_count, length, model_width)
    grad_low = cotangent.reshape(tokens, model_width)
    grad_down = token_outer(grad_low, activated)
    grad_act = jnp.dot(grad_low, down_weight, preferred_element_type=jnp.float32)
    gelu_back = jax.vjp(gelu_exact, pre_act)[1]
    grad_pre = gelu_back(grad_act)[0].astype(jnp.bfloat16)
    grad_up = token_outer(low_three, grad_pre)
    grad_normed = input_grad_sum(feature_inner(grad_pre, up_weight))
    norm_back = jax.vjp(layer_norm, resid_two, gain_rows[2])[1]
    grad_resid, grad_gain_three = norm_back(grad_normed)
    grad_two = grad_low.astype(jnp.float32) + grad_resid
    low_grad_two = grad_two.astype(jnp.bfloat16)
    grad_cross_out = token_outer(low_grad_two, cross_flat)
    grad_cross_mixed = (
        jnp.dot(low_grad_two, cross_out_weight, preferred_element_type=jnp.float32)
        .astype(jnp.bfloat16)
        .reshape(head_shape)
    )
    grad_cq, grad_ck, grad_cv = attend_back(
        cross_queries, row_kv[0], row_kv[1], None, score_scale, cross_total, grad_cross_mixed
    )
    low_cq = grad_cq.reshape(tokens, -1).astype(jnp.bfloat16)
    chooser = (image_ids[:, None] == jnp.arange(image_count)[None, :]).astype(jnp.float32)
    grad_rows_kv = jnp.stack([grad_ck, grad_cv]).reshape(2, row_count, context, -1)
    grad_image_kv = jnp.einsum(
        "ri,jrce->jice", chooser, grad_rows_kv, precision=lax.Precision.HIGHEST
    ).astype(jnp.bfloat16)
    grad_cross_query = token_outer(low_two, low_cq)
    grad_cross_kv = jnp.einsum(
        "ncd,jnce->jde", encoder, grad_image_kv, preferred_element_type=jnp.float32
    )
    encoder_part = jnp.einsum(
        "jnce,jde->ncd", grad_image_kv, cross_kv_weight, preferred_element_type=jnp.float32
    )
    encoder_grad = lax.psum_scatter(
        encoder_part.astype(jnp.bfloat16), "mp", scatter_dimension=2, tiled=True
    ).astype(jnp.float32)
    grad_normed = input_grad_sum(feature_inner(low_cq, cross_query_weight))
    norm_back = jax.vjp(layer_norm, resid_one, gain_rows[1])[1]
    grad_resid, grad_gain_two = norm_back(grad_normed)
    grad_one = grad_two + grad_resid
    low_grad_one = grad_one.astype(jnp.bfloat16)
    grad_self_out = token_outer(low_grad_one, self_flat)
    grad_self_mixed = (
        jnp.dot(low_grad_one, self_out_weight, preferred_element_type=jnp.float32)
        .astype(jnp.bfloat16)
        .reshape(head_shape)
    )
    grad_sq, grad_sk, grad_sv = attend_back(
        queries, key_heads, value_heads, allowed, score_scale, self_total, grad_self_mixed
    )
    grad_projected = (
        jnp.stack([grad_sq, grad_sk, grad_sv]).reshape(3, tokens, -1).astype(jnp.bfloat16)
    )
    grad_qkv = jnp.einsum(
        "td,jte->jde", low_one, grad_projected, preferred_element_type=jnp.float32
    )
    grad_normed = input_grad_sum(
        jnp.einsum("jte,jde->td", grad_projected, qkv_weight, preferred_element_type=jnp.float32)
    )
    norm_back = jax.vjp(layer_norm, flat_in, gain_rows[0])[1]
    grad_resid, grad_gain_one = norm_back(grad_normed)
    input_rows = (grad_one + grad_resid).reshape(row_count, length, model_width)
    grad_gains = jnp.stack([grad_gain_one, grad_gain_two, grad_gain_three])
    gradients = (
        grad_gains,
        grad_qkv,
        grad_self_out,
        grad_cross_query,
        grad_cross_kv,
        grad_cross_out,
        grad_up,
        grad_down,
    )
    return (output_rows, input_rows, encoder_grad, gradients)


def body(
    hidden,
    encoder_tokens,
    segment_ids,
    image_index,
    cotangent,
    norm_gains,
    qkv_weight,
    self_out_weight,
    cross_query_weight,
    cross_kv_weight,
    cross_out_weight,
    up_weight,
    down_weight,
):
    micro_count = hidden.shape[0]
    gathered = None
    outputs = []
    input_grads = []
    encoder_grads = []
    reduced = None
    for micro_index in range(micro_count):
        gathered = fetch_weights(
            norm_gains,
            qkv_weight,
            self_out_weight,
            cross_query_weight,
            cross_kv_weight,
            cross_out_weight,
            up_weight,
            down_weight,
        )
        output_rows, input_rows, encoder_rows, gradients = micro_step(
            gathered,
            hidden[micro_index],
            encoder_tokens[micro_index],
            segment_ids[micro_index],
            image_index[micro_index],
            cotangent[micro_index],
        )
        outputs.append(output_rows)
        input_grads.append(input_rows)
        encoder_grads.append(encoder_rows)
        shards = reduce_weight_grads(gradients)
        reduced = shards if reduced is None else jax.tree.map(add_pair, reduced, shards)
    return (
        jnp.stack(outputs),
        jnp.stack(input_grads),
        jnp.stack(encoder_grads),
        reduced[0],
        reduced[1],
        reduced[2],
        reduced[3],
        reduced[4],
        reduced[5],
        reduced[6],
        reduced[7],
    )


def solution(mesh):
    placed = (
        P(None, "dp", None, None),
        P(None, "dp", None, None),
        P(None, "dp", None),
        P(None, "dp"),
        P(None, "dp", None, None),
        P(None, "dp"),
        P(None, "dp", "mp"),
        P("dp", "mp"),
        P("dp", "mp"),
        P(None, "dp", "mp"),
        P("dp", "mp"),
        P("dp", "mp"),
        P("dp", "mp"),
    )
    return jax.shard_map(
        body,
        mesh=mesh,
        in_specs=placed,
        out_specs=(
            P(None, "dp", None, None),
            P(None, "dp", None, None),
            P(None, "dp", None, "mp"),
            P(None, "dp"),
            P(None, "dp", "mp"),
            P("dp", "mp"),
            P("dp", "mp"),
            P(None, "dp", "mp"),
            P("dp", "mp"),
            P("dp", "mp"),
            P("dp", "mp"),
        ),
        check_vma=False,
    )
```

profile of v0, /device:TPU:0, one launch (start us, length us, event | category | flops | bytes accessed | tf_op | source)
XLA Modules:
  0.0 1708.3 jit_solution(6245522283395078489)
XLA Ops:
  11.9 42.4 %all-gather = bf16[16,48,3]{1,2,0:T(4,128)(2,1)S(1)} all-gather(bf16[1,48,3]{1,2,0:T(4,128)(2,1)S(1)} %bitcast.350), channel_id=1, replica_groups=mesh['dp'=16,'mp'=2] {'dp'}, dimensions={0}, use_global_device_ids=true | all-gather | bytes 4896 | tf_op jit(solution)/shard_map/all_gather | solution.py:93
  56.9 40.3 %all_gather.34 = bf16[768,384]{1,0:T(8,128)(2,1)S(1)} all-gather(bf16[48,384]{1,0:T(8,128)(2,1)S(1)} %copy-done.100), channel_id=1, replica_groups=mesh['dp'=16,'mp'=2] {'dp'}, dimensions={0}, use_global_device_ids=true | all-gather | bytes 626688 | tf_op jit(solution)/shard_map/all_gather | solution.py:95
  97.3 44.4 %all_gather.36 = bf16[768,384]{1,0:T(8,128)(2,1)} all-gather(bf16[48,384]{1,0:T(8,128)(2,1)S(1)} %copy-done.101), channel_id=1, replica_groups=mesh['dp'=16,'mp'=2] {'dp'}, dimensions={0}, use_global_device_ids=true | all-gather | bytes 626688 | tf_op jit(solution)/shard_map/all_gather | solution.py:96
  141.7 40.7 %all_gather.37 = bf16[768,384]{1,0:T(8,128)(2,1)S(1)} all-gather(bf16[48,384]{1,0:T(8,128)(2,1)S(1)} %copy-done.102), channel_id=1, replica_groups=mesh['dp'=16,'mp'=2] {'dp'}, dimensions={0}, use_global_device_ids=true | all-gather | bytes 626688 | tf_op jit(solution)/shard_map/all_gather | solution.py:98
  182.4 4.8 convert_bitcast_fusion
  187.2 4.3 gather_fusion.1
  219.5 4.0 copy.281
  223.5 4.2 convert_bitcast_fusion.1
  227.7 4.4 gather_fusion
  236.8 3.9 copy.268
  240.7 3.9 copy.266
  281.2 14.4 all-reduce.21.cloned.1.call-done
  300.1 61.7 %all-gather.10.cloned.1.call-done = bf16[768,1536]{1,0:T(8,128)(2,1)} async-done(((bf16[48,1536]{1,0:T(8,128)(2,1)}), bf16[768,1536]{1,0:T(8,128)(2,1)}) %all-gather.10.cloned.1.call-update) | async-done | bytes 2359312 | tf_op jit(solution)/shard_map/all_gather | solution.py:99
  361.8 3.9 fusion.192
  365.7 59.9 %all-gather.12.cloned.1.call-done = bf16[768,1536]{1,0:T(8,128)(2,1)} async-done(((bf16[48,1536]{1,0:T(8,128)(2,1)}), bf16[768,1536]{1,0:T(8,128)(2,1)}) %all-gather.12.cloned.1.call-update) | async-done | bytes 2359312 | tf_op jit(solution)/shard_map/all_gather | solution.py:100
  425.6 6.4 add_convert_fusion
  437.4 5.1 add_convert_fusion.1
  456.9 6.3 all-reduce.29.cloned.1.call-done
  468.4 19.6 %all-reduce.19.cloned.1.call-done = (f32[256,768]{1,0:T(8,128)}, f32[256,768]{1,0:T(8,128)}) async-done(((f32[256,768]{1,0:T(8,128)}, f32[256,768]{1,0:T(8,128)}), (f32[256,768]{1,0:T(8,128)}, f32[256,768]{1,0:T(8,128)})) %all-reduce.19.cloned.1.call-update) | async-done | bytes 1572880 | tf_op jit(solution)/shard_map/psum | solution.py:118
  506.9 4.5 multiply_reduce_fusion.1
  521.5 4.5 multiply_reduce_fusion
  541.5 5.1 fusion.27
  546.6 6.3 copy.329
  618.4 4.3 convolution_multiply_fusion.1
  622.6 6.2 copy.328
  628.8 10.9 fusion.16
  649.2 4.7 bitcast_convert_fusion.1
  653.9 6.6 copy.374
  660.4 5.0 reshape.449
  665.6 5.0 fusion.25
  670.6 6.1 copy.334
  676.7 4.2 convolution_multiply_fusion
  681.0 6.2 copy.333
  687.1 10.1 fusion.19
  701.3 6.6 copy.376
  707.8 5.0 reshape.451
  713.1 3.9 fusion.35
  720.3 5.3 copy.341
  730.1 6.2 copy.338
  757.0 6.1 copy.380
  773.5 9.2 reduce-scatter.25.cloned.1.call-done
  787.2 8.2 reduce-scatter.27.cloned.1.call-done
  801.9 229.5 %all-reduce.17.cloned.1.call-done = (f32[3,768,384]{2,0,1:T(4,128)}, f32[2,768,384]{2,0,1:T(2,128)}) async-done(((f32[3,768,384]{2,0,1:T(4,128)}, f32[2,768,384]{2,0,1:T(2,128)}), (f32[3,768,384]{2,0,1:T(4,128)}, f32[2,768,384]{2,0,1:T(2,128)})) %all-reduce.17.cloned.1.call-update) | async-done | bytes 5898256
  1034.8 125.2 %reduce-scatter.21.cloned.1.call-done = f32[48,384]{1,0:T(8,128)} async-done(((f32[768,384]{1,0:T(8,128)}), f32[48,384]{1,0:T(8,128)}) %reduce-scatter.21.cloned.1.call-update) | async-done | bytes 73744 | tf_op jit(solution)/shard_map/reduce_scatter | solution.py:111
  1159.9 128.6 %reduce-scatter.19.cloned.1.call-done = f32[48,384]{1,0:T(8,128)} async-done(((f32[768,384]{1,0:T(8,128)}), f32[48,384]{1,0:T(8,128)}) %reduce-scatter.19.cloned.1.call-update) | async-done | bytes 73744 | tf_op jit(solution)/shard_map/reduce_scatter | solution.py:109
  1288.5 128.5 %reduce-scatter.17.cloned.1.call-done = f32[48,384]{1,0:T(8,128)} async-done(((f32[768,384]{1,0:T(8,128)}), f32[48,384]{1,0:T(8,128)}) %reduce-scatter.17.cloned.1.call-update) | async-done | bytes 73744 | tf_op jit(solution)/shard_map/reduce_scatter | solution.py:108
  1417.0 142.4 %reduce-scatter.23.cloned.1.call-done = f32[48,1536]{1,0:T(8,128)} async-done(((f32[768,1536]{1,0:T(8,128)}), f32[48,1536]{1,0:T(8,128)}) %reduce-scatter.23.cloned.1.call-update) | async-done | bytes 294928 | tf_op jit(solution)/shard_map/reduce_scatter | solution.py:112
  1559.5 141.9 %reduce-scatter.31.cloned.1.call-done = f32[48,1536]{1,0:T(8,128)} async-done(((f32[768,1536]{1,0:T(8,128)}), f32[48,1536]{1,0:T(8,128)}) %reduce-scatter.31.cloned.1.call-update) | async-done | bytes 294928
  (538 shorter events, 280.6 us)
Async XLA Ops:
  7.2 48.7 %copy-start.4 = (bf16[2,4,64,768]{3,2,1,0:T(8,128)(2,1)S(1)}, bf16[2,4,64,768]{3,2,1,0:T(8,128)(2,1)}, u32[]{:S(2)}) copy-start(bf16[2,4,64,768]{3,2,1,0:T(8,128)(2,1)} %param.15) | copy-start | bytes 2359300
  7.2 47.3 %copy-start.130 = (s32[2,4]{1,0:T(2,128)S(1)}, s32[2,4]{1,0:T(2,128)}, u32[]{:S(2)}) copy-start(s32[2,4]{1,0:T(2,128)} %param.18) | copy-start | bytes 100
  7.2 47.9 %copy-start.131 = (s32[2,4,64]{2,1,0:T(4,128)S(1)}, s32[2,4,64]{2,1,0:T(4,128)}, u32[]{:S(2)}) copy-start(s32[2,4,64]{2,1,0:T(4,128)} %param.17) | copy-start | bytes 6148
  7.2 175.2 %all-gather.8.cloned.1.call-start = ((), (), s32[]{:S(2)}) async-start(), calls=%async_computation.9 | async-start | bytes 1253376 | tf_op jit(solution)/shard_map/all_gather | solution.py:97
  8.0 49.0 %copy-start.100 = (bf16[48,384]{1,0:T(8,128)(2,1)S(1)}, bf16[48,384]{1,0:T(8,128)(2,1)}, u32[]{:S(2)}) copy-start(bf16[48,384]{1,0:T(8,128)(2,1)} %param.22) | copy-start | bytes 110596
  8.0 183.6 %all-gather.6.cloned.1.call-start = ((), (), s32[]{:S(2)}) async-start(), calls=%async_computation.8 | async-start | bytes 1880064 | tf_op jit(solution)/shard_map/all_gather | solution.py:94
  8.7 239.7 %all-reduce.23.cloned.1.call-start = ((), (), s32[]{:S(2)}) async-start(), calls=%async_computation.23 | async-start | bytes 3145728 | tf_op jit(solution)/shard_map/psum | solution.py:118
  10.1 87.2 %copy-start.101 = (bf16[48,384]{1,0:T(8,128)(2,1)S(1)}, bf16[48,384]{1,0:T(8,128)(2,1)}, u32[]{:S(2)}) copy-start(bf16[48,384]{1,0:T(8,128)(2,1)} %param.23) | copy-start | bytes 110596
  10.1 131.6 %copy-start.102 = (bf16[48,384]{1,0:T(8,128)(2,1)S(1)}, bf16[48,384]{1,0:T(8,128)(2,1)}, u32[]{:S(2)}) copy-start(bf16[48,384]{1,0:T(8,128)(2,1)} %param.25) | copy-start | bytes 110596
  11.7 170.7 %copy-start.107 = (f32[256]{0:T(256)}, f32[256]{0:T(256)S(1)}, u32[]{:S(2)}) copy-start(f32[256]{0:T(256)S(1)} %div.157) | copy-start | bytes 3076
  11.7 170.6 %copy-start.109 = (f32[256]{0:T(256)}, f32[256]{0:T(256)S(1)}, u32[]{:S(2)}) copy-start(f32[256]{0:T(256)S(1)} %div.168) | copy-start | bytes 3076
  11.8 43.2 %copy-start.123 = (f32[256]{0:T(256)}, f32[256]{0:T(256)S(1)}, u32[]{:S(2)}) copy-start(f32[256]{0:T(256)S(1)} %add.228) | copy-start | bytes 3076
  11.8 170.5 %copy-start.113 = (f32[256]{0:T(256)}, f32[256]{0:T(256)S(1)}, u32[]{:S(2)}) copy-start(f32[256]{0:T(256)S(1)} %rsqrt.66) | copy-start | bytes 3076
  11.9 43.1 %copy-start.124 = (f32[256]{0:T(256)}, f32[256]{0:T(256)S(1)}, u32[]{:S(2)}) copy-start(f32[256]{0:T(256)S(1)} %add.235) | copy-start | bytes 3076
  11.9 170.4 %copy-start.115 = (f32[256]{0:T(256)}, f32[256]{0:T(256)S(1)}, u32[]{:S(2)}) copy-start(f32[256]{0:T(256)S(1)} %rsqrt.69) | copy-start | bytes 3076
  56.9 134.6 %copy-start.67 = (bf16[256,768]{1,0:T(8,128)(2,1)}, bf16[256,768]{1,0:T(8,128)(2,1)S(1)}, u32[]{:S(2)}) copy-start(bf16[256,768]{1,0:T(8,128)(2,1)S(1)} %get-tuple-element.120) | copy-start | bytes 1179652
  97.3 115.6 %copy-start.15 = (bf16[768,384]{1,0:T(8,128)(2,1)}, bf16[768,384]{1,0:T(8,128)(2,1)S(1)}, u32[]{:S(2)}) copy-start(bf16[768,384]{1,0:T(8,128)(2,1)S(1)} %all_gather.34) | copy-start | bytes 1769476
  182.4 95.4 %copy-start.18 = (bf16[768,384]{1,0:T(8,128)(2,1)}, bf16[768,384]{1,0:T(8,128)(2,1)S(1)}, u32[]{:S(2)}) copy-start(bf16[768,384]{1,0:T(8,128)(2,1)S(1)} %all_gather.37) | copy-start | bytes 1769476
  195.5 12.4 copy-start.43
  214.2 81.4 %all-reduce.21.cloned.1.call-start = ((), (), s32[]{:S(2)}) async-start(), calls=%async_computation.22 | async-start | bytes 3145728 | tf_op jit(solution)/shard_map/psum | solution.py:118
  254.6 12.4 copy-start.40
  266.9 9.6 copy-start.61
  279.1 82.6 %all-gather.10.cloned.1.call-start = ((), (), s32[]{:S(2)}) async-start(), calls=%async_computation.10 | async-start | bytes 2506752 | tf_op jit(solution)/shard_map/all_gather | solution.py:99
  279.7 145.8 %all-gather.12.cloned.1.call-start = ((), (), s32[]{:S(2)}) async-start(), calls=%async_computation.11 | async-start | bytes 2506752 | tf_op jit(solution)/shard_map/all_gather | solution.py:100
  280.3 183.0 %all-reduce.29.cloned.1.call-start = ((), (), s32[]{:S(2)}) async-start(), calls=%async_computation.26 | async-start | bytes 1572864 | tf_op jit(solution)/shard_map/psum | solution.py:122
  425.6 6.4 copy-start.34
  445.0 43.0 %all-reduce.19.cloned.1.call-start = ((), (), s32[]{:S(2)}) async-start(), calls=%async_computation.21 | async-start | bytes 3145728 | tf_op jit(solution)/shard_map/psum | solution.py:118
  452.7 104.1 %all-reduce.27.cloned.1.call-start = ((), (), s32[]{:S(2)}) async-start(), calls=%async_computation.25 | async-start | bytes 1572864 | tf_op jit(solution)/shard_map/psum | solution.py:122
  488.0 5.5 copy-start.19
  536.2 104.7 %all-reduce.25.cloned.1.call-start = ((), (), s32[]{:S(2)}) async-start(), calls=%async_computation.24 | async-start | bytes 1572864 | tf_op jit(solution)/shard_map/psum | solution.py:122
  617.9 154.1 %reduce-scatter.29.cloned.1.call-start = ((), (), s32[]{:S(2)}) async-start(), calls=%async_computation.18 | async-start | bytes 417792
  628.8 10.9 copy-start.111
  628.8 11.5 copy-start.112
  649.1 133.5 %reduce-scatter.25.cloned.1.call-start = ((), (), s32[]{:S(2)}) async-start(), calls=%async_computation.16 | async-start | bytes 2654208
  665.4 130.0 %reduce-scatter.27.cloned.1.call-start = ((), (), s32[]{:S(2)}) async-start(), calls=%async_computation.17 | async-start | bytes 2654208
  687.1 11.3 copy-start.140
  712.8 318.6 %all-reduce.17.cloned.1.call-start = ((), (), s32[]{:S(2)}) async-start(), calls=%async_computation.20 | async-start | bytes 14155776
  736.4 423.6 %reduce-scatter.21.cloned.1.call-start = ((), (), s32[]{:S(2)}) async-start(), calls=%async_computation.14 | async-start | bytes 1253376 | tf_op jit(solution)/shard_map/reduce_scatter | solution.py:111
  739.4 549.1 %reduce-scatter.19.cloned.1.call-start = ((), (), s32[]{:S(2)}) async-start(), calls=%async_computation.13 | async-start | bytes 1253376 | tf_op jit(solution)/shard_map/reduce_scatter | solution.py:109
  743.4 673.6 %reduce-scatter.17.cloned.1.call-start = ((), (), s32[]{:S(2)}) async-start(), calls=%async_computation.12 | async-start | bytes 1253376 | tf_op jit(solution)/shard_map/reduce_scatter | solution.py:108
  746.4 813.1 %reduce-scatter.23.cloned.1.call-start = ((), (), s32[]{:S(2)}) async-start(), calls=%async_computation.15 | async-start | bytes 5013504 | tf_op jit(solution)/shard_map/reduce_scatter | solution.py:112
  751.8 949.5 %reduce-scatter.31.cloned.1.call-start = ((), (), s32[]{:S(2)}) async-start(), calls=%async_computation.19 | async-start | bytes 5013504
  763.1 5.4 copy-start.108
  763.1 5.4 copy-start.110
  763.1 5.4 copy-start.114
  763.1 5.4 copy-start.25
  763.2 5.4 copy-start.54
  763.2 5.4 copy-start.56
  (114 other events, 277.9 us)
Sparse Core Ops, SparseCore 0:
  10.7 59.4 all-gather.7
  72.9 61.2 all-gather.5
  214.3 16.3 all-reduce.22
  279.2 16.3 all-reduce.20
  298.3 63.4 all-gather.9
  364.4 61.0 all-gather.11
  445.1 18.0 all-reduce.28
  466.3 21.6 all-reduce.18
  536.3 20.4 all-reduce.26
  618.0 20.4 all-reduce.24
  649.3 122.7 reduce-scatter.28
  774.3 8.3 reduce-scatter.24
  784.9 10.4 reduce-scatter.26
  802.8 228.5 all-reduce.16
  1037.3 122.5 reduce-scatter.20
  1165.8 122.6 reduce-scatter.18
  1294.4 122.5 reduce-scatter.16
  1423.4 135.9 reduce-scatter.22
  1565.2 136.0 reduce-scatter.30
where the time goes:
time: 1720 us; the launch traced here: 1710 us
  waiting for transfers between devices  1080 us (63%)
  local copies, waits for them, and re-layouts  209 us (12%)
  matrix products  169 us (10%)
  blocking collectives  168 us (10%)
  other arithmetic  59.6 us (3%)
    unnamed x24, waiting for transfers between devices  392 us
    reduce_scatter x1, waiting for transfers between devices, reduce_weight_grads(): lax.psum_scatter(gradients[6], 'dp', scatter_dimension=0, tiled=True)  142 us
    reduce_scatter x1, waiting for transfers between devices, reduce_weight_grads(): lax.psum_scatter(gradients[3], 'dp', scatter_dimension=0, tiled=True)  129 us
    reduce_scatter x1, waiting for transfers between devices, reduce_weight_grads(): lax.psum_scatter(gradients[2], 'dp', scatter_dimension=0, tiled=True)  128 us
    reduce_scatter x1, waiting for transfers between devices, reduce_weight_grads(): lax.psum_scatter(gradients[5], 'dp', scatter_dimension=0, tiled=True)  125 us
    unnamed x306, local copies, waits for them, and re-layouts  68.8 us
    all_gather x1, waiting for transfers between devices, fetch_weights(): lax.all_gather(up_weight, 'dp', axis=0, tiled=True)  61.7 us
    all_gather x1, waiting for transfers between devices, fetch_weights(): lax.all_gather(down_weight, 'dp', axis=0, tiled=True)  59.9 us
  transfers between devices with their start and end apart: 19, of which 15 were waited for; matrix products, arithmetic and copies ran while one was open for 14% of the time, Pallas kernels for 0%

commit v1 on v0

v1 whole, which is shorter than its diff:
```python
import functools
from types import SimpleNamespace

import jax
import jax.numpy as jnp
from jax import lax
from jax.experimental import pallas as pl
from jax.experimental.pallas import tpu as pltpu
from jax.sharding import PartitionSpec as P

HEAD = 64
PAIR = 2 * HEAD
EPSILON = 1e-05
NEGATIVE = -1e30
ROOT_HALF = 0.7071067811865476
DENSITY = 0.3989422804014327
MESH = pl.DeviceIdType.MESH
LOW = jnp.bfloat16
F32 = jnp.float32
QKV, SO, CQ, CKV, CO, MATS = 0, 3, 4, 5, 7, 8
UP, DOWN = 0, 1
LN_ROWS = 64
TILE = 256


def dot(left, right, left_dim, right_dim):
    return lax.dot_general(
        left, right, (((left_dim,), (right_dim,)), ((), ())), preferred_element_type=F32
    )


def lanes_of(pair):
    return pl.ds(pair * PAIR, PAIR)


def head_masks():
    lane = lax.broadcasted_iota(jnp.int32, (1, PAIR), 1)
    first = jnp.where(lane < HEAD, 1.0, 0.0)
    return first.astype(LOW), (1.0 - first).astype(LOW)


def stack_heads(values, masks):
    return jnp.concatenate([values * masks[0], values * masks[1]], axis=0)


def join_heads(stacked):
    half = stacked.shape[0] // 2
    lane = lax.broadcasted_iota(jnp.int32, (half, PAIR), 1)
    return jnp.where(lane < HEAD, stacked[:half], stacked[half:])


def centre(values):
    centred = values - jnp.mean(values, axis=-1, keepdims=True)
    spread = jnp.mean(centred * centred, axis=-1, keepdims=True)
    scale = lax.rsqrt(spread + EPSILON)
    return centred * scale, scale


def softmax_keys(scores):
    shifted = jnp.exp(scores - jnp.max(scores, axis=0, keepdims=True))
    return shifted / jnp.sum(shifted, axis=0, keepdims=True)


def layer(g, *refs):
    r = SimpleNamespace(**dict(zip(g.names, refs)))
    me, mp = lax.axis_index("dp"), lax.axis_index("mp")
    zi, col = me // 4, me % 4
    sibling = (me, 1 - mp)
    col_x = col + 1 - 2 * (col % 2)
    col_y = (col + 2) % 4
    col_d = (col_x + 2) % 4
    col_a = mp * col_x + (1 - mp) * col_y
    col_b = mp * col_y + (1 - mp) * col_x
    at_x, at_y = (zi * 4 + col_x, mp), (zi * 4 + col_y, mp)
    at_a, at_b = (zi * 4 + col_a, mp), (zi * 4 + col_b, mp)
    z_of = [(zi + k) % g.nz for k in range(1, g.nz)]
    z_from = [(zi + g.nz - k) % g.nz for k in range(1, g.nz)]
    at_z = [(z * 4 + col, mp) for z in z_of]

    greeted = [sibling] + ([at_x, at_y] + at_z if g.comm else [])
    barrier = pltpu.get_barrier_semaphore()
    for device in greeted:
        pl.semaphore_signal(barrier, inc=1, device_id=device, device_id_type=MESH)

    def remote(src, dst, send, recv, device):
        return pltpu.make_async_remote_copy(
            src_ref=src, dst_ref=dst, send_sem=send, recv_sem=recv, device_id=device, device_id_type=MESH
        )

    def own(matrices, block=None):
        if not g.comm:
            return matrices
        return matrices.at[:, zi, col] if block is None else block

    local = []

    def bring(src, dst):
        copy = pltpu.make_async_copy(src, dst, r.local_sem.at[len(local)])
        copy.start()
        local.append(copy)
        return copy

    def slot(first, count):
        ref = r.w8.at[pl.ds(first, count)]
        return ref.at[:, zi, col] if g.comm else ref

    def wide_slot(which):
        return r.wf.at[which, zi, col] if g.comm else r.wf.at[which]

    weights = [
        bring(r.qkv_in, slot(QKV, 3)),
        bring(r.so_in, slot(SO, 1)),
        bring(r.cq_in, slot(CQ, 1)),
        bring(r.ckv_in, slot(CKV, 2)),
        bring(r.co_in, slot(CO, 1)),
        bring(r.up_in, wide_slot(UP)),
        bring(r.down_in, wide_slot(DOWN)),
    ]
    bring_enc = bring(r.enc_in, r.enc)
    bring_cot = bring(r.cot_in, r.cot)

    half = g.ff // 2
    gather_groups = [
        ("8", QKV, 3), ("8", SO, 2), ("8", CKV, 2), ("8", CO, 1),
        ("f", UP, 0), ("f", UP, half), ("f", DOWN, 0), ("f", DOWN, half),
    ]
    reduce_groups = [
        ("f", DOWN, 0), ("f", DOWN, half), ("f", UP, 0), ("f", UP, half),
        ("8", CO, 1), ("8", CKV, 2), ("8", CQ, 1), ("8", SO, 1), ("8", QKV, 3),
    ]

    def block_of(group, small, wide, z, c):
        kind, first, more = group
        if kind == "8":
            return small.at[pl.ds(first, more), z, c]
        return wide.at[first, z, c, :, pl.ds(more, half)]

    def column_of(group, small, wide, c):
        kind, first, more = group
        if kind == "8":
            return small.at[pl.ds(first, more), :, c]
        return wide.at[first, :, c, :, pl.ds(more, half)]

    started = []

    def start(copy):
        copy.start()
        started.append(copy)

    def gather_z(i):
        group = gather_groups[i]
        for k in range(g.nz - 1):
            block = block_of(group, r.w8, r.wf, zi, col)
            start(remote(block, block, r.agz_s.at[i, k], r.agz_r.at[i, k], at_z[k]))

    def gather_ab(i):
        group = gather_groups[i]
        for k in range(g.nz - 1):
            block = block_of(group, r.w8, r.wf, z_from[k], col)
            remote(block, block, r.agz_s.at[i, k], r.agz_r.at[i, k], at_z[k]).wait_recv()
        column = column_of(group, r.w8, r.wf, col)
        start(remote(column, column, r.aga_s.at[i], r.aga_r.at[i], at_a))
        start(remote(column, column, r.agb_s.at[i, 0], r.agb_r.at[i, 0], at_b))

    def gather_b(i):
        column = column_of(gather_groups[i], r.w8, r.wf, col_a)
        remote(column, column, r.aga_s.at[i], r.aga_r.at[i], at_a).wait_recv()
        start(remote(column, column, r.agb_s.at[i, 1], r.agb_r.at[i, 1], at_b))

    def gather_end(i):
        for k, c in enumerate((col_b, col_d)):
            column = column_of(gather_groups[i], r.w8, r.wf, c)
            remote(column, column, r.agb_s.at[i, k], r.agb_r.at[i, k], at_b).wait_recv()

    def reduce_b(i):
        group = reduce_groups[i]
        for k, c in enumerate((col_b, col_d)):
            start(remote(
                column_of(group, r.p8, r.pf, c), column_of(group, r.lb8.at[k], r.lbf.at[k], 0),
                r.rsb_s.at[i, k], r.rsb_r.at[i, k], at_b,
            ))

    def each_block(group, body):
        kind, first, more = group
        if kind == "8":
            for j in range(first, first + more):
                @pl.loop(0, g.nz)
                def _(z):
                    body(lambda small, wide, c: small.at[j, z, c])
        else:
            @pl.loop(0, g.nz)
            def _(z):
                body(lambda small, wide, c: wide.at[first, z, c, :, pl.ds(more, half)])

    def add_into(group, c, small, wide):
        def body(view):
            target, landed = view(r.p8, r.pf, c), view(small, wide, 0)
            total = target[...].astype(F32) + landed[...].astype(F32)
            target[...] = total.astype(LOW)
        each_block(group, body)

    def reduce_a(i):
        group = reduce_groups[i]
        for k in (1, 0):
            landed = column_of(group, r.lb8.at[k], r.lbf.at[k], 0)
            remote(landed, landed, r.rsb_s.at[i, k], r.rsb_r.at[i, k], at_b).wait_recv()
            add_into(group, (col, col_a)[k], r.lb8.at[k], r.lbf.at[k])
            if k:
                start(remote(
                    column_of(group, r.p8, r.pf, col_a), column_of(group, r.la8, r.laf, 0),
                    r.rsa_s.at[i], r.rsa_r.at[i], at_a,
                ))

    def reduce_z(i):
        group = reduce_groups[i]
        landed = column_of(group, r.la8, r.laf, 0)
        remote(landed, landed, r.rsa_s.at[i], r.rsa_r.at[i], at_a).wait_recv()
        add_into(group, col, r.la8, r.laf)
        for k in range(g.nz - 1):
            start(remote(
                block_of(group, r.p8, r.pf, z_of[k], col), block_of(group, r.lz8, r.lzf, k, 0),
                r.rsz_s.at[i, k], r.rsz_r.at[i, k], at_z[k],
            ))

    def reduce_end(i):
        kind, first, more = reduce_groups[i]
        for k in range(g.nz - 1):
            landed = block_of(reduce_groups[i], r.lz8, r.lzf, k, 0)
            remote(landed, landed, r.rsz_s.at[i, k], r.rsz_r.at[i, k], at_z[k]).wait_recv()
        if kind == "8":
            for j in range(first, first + more):
                total = r.p8[j, zi, col].astype(F32)
                for k in range(g.nz - 1):
                    total = total + r.lz8[j, k, 0].astype(F32)
                r.g8_out[j] = total
        else:
            cols = pl.ds(more, half)
            total = r.pf[first, zi, col, :, cols].astype(F32)
            for k in range(g.nz - 1):
                total = total + r.lzf[first, k, 0, :, cols].astype(F32)
            r.gf_out[first, :, cols] = total

    n_reduce = len(reduce_groups)

    def reduce_start(i):
        if not g.comm:
            return
        if i < n_reduce:
            reduce_b(i)
        if 0 <= i - 3 < n_reduce:
            reduce_end(i - 3)
        if 0 <= i - 2 < n_reduce:
            reduce_z(i - 2)
        if 0 <= i - 1 < n_reduce:
            reduce_a(i - 1)

    def w8(j):
        return r.w8[j].reshape(g.d, g.f)

    def wide(which, cols):
        if g.comm:
            return r.wf[which, :, :, :, cols].reshape(g.d, -1)
        return r.wf[which, :, cols]

    def put8(j, value):
        r.p8[j] = value.astype(LOW).reshape(r.p8.shape[1:])

    def put_wide(which, cols, value):
        if g.comm:
            r.pf[which, :, :, :, cols] = value.astype(LOW).reshape(g.nz, 4, g.blk, -1)
        else:
            r.pf[which, :, cols] = value.astype(LOW)

    part = g.t // 2

    def exchange(e, i):
        rows = pl.ds(i * part, part)
        return remote(
            r.stage.at[e % 2, rows], r.land.at[e % 3, rows], r.ex_s.at[e, i], r.ex_r.at[e, i], sibling
        )

    def exchange_start(e, product):
        for i in range(2):
            rows = pl.ds(i * part, part)
            r.stage[e % 2, rows] = product(rows).astype(LOW)
            exchange(e, i).start()

    def by_rows(e, body):
        for i in range(2):
            exchange(e, i).wait_recv()
            exchange(e, i).wait_send()

            @pl.loop(0, part // LN_ROWS)
            def _(n):
                rows = pl.ds(pl.multiple_of(i * part + n * LN_ROWS, LN_ROWS), LN_ROWS)
                body(rows, r.stage[e % 2, rows].astype(F32) + r.land[e % 3, rows].astype(F32))

    def norm(values, i):
        return (centre(values)[0] * r.gains[i]).astype(LOW)

    def norm_back(i, values, grad):
        normed, scale = centre(values)
        r.gain_sum[i] += jnp.sum((grad * normed).reshape(-1, 8, g.d), axis=0)
        scaled = grad * r.gains[i]
        return scale * (
            scaled
            - jnp.mean(scaled, axis=-1, keepdims=True)
            - normed * jnp.mean(scaled * normed, axis=-1, keepdims=True)
        )

    masks = head_masks()
    score_scale = HEAD ** (-0.5)
    pairs = g.f // PAIR

    pl.semaphore_wait(barrier, len(greeted))
    small = []

    def meet(src, dst, i, device):
        copy = remote(src, dst, r.small_s.at[i], r.small_r.at[i], device)
        copy.start()
        small.append(copy)
        return copy

    if g.comm:
        for k in range(g.nz - 1):
            meet(r.gains_in, r.gain_land.at[k], k, at_z[k])
        weights[0].wait()
        gather_z(0)
        weights[1].wait()
        weights[2].wait()
        gather_z(1)
        for k in range(g.nz - 1):
            small[k].wait_recv()
        total = r.gains_in[...].astype(F32)
        for k in range(g.nz - 1):
            total = total + r.gain_land[k].astype(F32)
        r.gain_pass[0] = total.astype(LOW)
        meet(r.gain_pass.at[0], r.gain_land.at[g.nz - 1], g.nz - 1, at_x).wait_recv()
        total = total + r.gain_land[g.nz - 1].astype(F32)
        r.gain_pass[1] = total.astype(LOW)
        meet(r.gain_pass.at[1], r.gain_land.at[g.nz], g.nz, at_y).wait_recv()
        total = total + r.gain_land[g.nz].astype(F32)
        for copy in weights[3:]:
            copy.wait()
    else:
        total = r.gains_in[...].astype(F32)
        for copy in weights:
            copy.wait()
    for i in range(3):
        r.gains[i] = total[i:i + 1]

    def gather_steps(*steps):
        if g.comm:
            for step, i in steps:
                step(i)

    gather_steps((gather_ab, 0), (gather_z, 2))

    r.gain_sum[...] = jnp.zeros_like(r.gain_sum)

    @pl.loop(0, g.t // LN_ROWS)
    def _(n):
        rows = pl.ds(pl.multiple_of(n * LN_ROWS, LN_ROWS), LN_ROWS)
        r.a1[rows] = norm(r.hidden[rows].astype(F32), 0)

    seg_down = r.seg[...].T
    for p in range(g.t // PAIR):
        key = lax.broadcasted_iota(jnp.int32, (PAIR, PAIR), 0)
        query = lax.broadcasted_iota(jnp.int32, (PAIR, PAIR), 1)
        allowed = (key <= query) & (seg_down[:, p:p + 1] == r.seg[p:p + 1, :])
        r.bias[p] = jnp.where(allowed, 0.0, NEGATIVE)

    gather_steps((gather_b, 0), (gather_ab, 1), (gather_z, 3), (gather_end, 0), (gather_b, 1), (gather_ab, 2), (gather_z, 4))
    for j in range(3):
        r.qkv[j] = dot(r.a1[...], w8(QKV + j), 1, 0).astype(LOW)

    @pl.loop(0, g.t // PAIR)
    def _(p):
        rows = pl.ds(pl.multiple_of(p * PAIR, PAIR), PAIR)
        bias = jnp.concatenate([r.bias[p]] * 2, axis=1)
        for h in range(pairs):
            lanes = lanes_of(h)
            queries = stack_heads(r.qkv[0, rows, lanes], masks)
            scores = dot(r.qkv[1, rows, lanes], queries, 1, 1) * score_scale + bias
            weights_low = softmax_keys(scores).astype(LOW)
            r.self_p[p, h] = weights_low
            r.mixed[rows, lanes] = join_heads(dot(weights_low, r.qkv[2, rows, lanes], 0, 0)).astype(LOW)

    gather_steps((gather_end, 1), (gather_b, 2), (gather_ab, 3), (gather_z, 5))
    exchange_start(0, lambda rows: dot(r.mixed[rows], w8(SO), 1, 1))

    def after_self(rows, total):
        resid = r.hidden[rows].astype(F32) + total
        r.resid_one[rows] = resid
        r.a2[rows] = norm(resid, 1)

    by_rows(0, after_self)
    r.cq[...] = dot(r.a2[...], w8(CQ), 1, 0).astype(LOW)

    gather_steps((gather_end, 2), (gather_b, 3), (gather_ab, 4), (gather_z, 6))
    bring_enc.wait()
    for m in range(2):
        for image in range(g.images):
            rows = pl.ds(image * g.ctx, g.ctx)
            r.kv[m, image] = dot(r.enc[rows], w8(CKV + m), 1, 0).astype(LOW)
        if m == 0:
            gather_steps((gather_b, 4), (gather_ab, 5), (gather_z, 7))

    @pl.loop(0, g.rows)
    def _(row):
        rows = pl.ds(pl.multiple_of(row * g.seq, g.seq), g.seq)
        image = (row // g.row_mb) * g.img_mb + r.image_ids[row]
        for h in range(pairs):
            lanes = lanes_of(h)
            queries = stack_heads(r.cq[rows, lanes], masks)
            scores = dot(r.kv[0, image, :, lanes], queries, 1, 1) * score_scale
            weights_low = softmax_keys(scores).astype(LOW)
            r.cross_p[row * pairs + h] = weights_low
            r.cmixed[rows, lanes] = join_heads(dot(weights_low, r.kv[1, image, :, lanes], 0, 0)).astype(LOW)

    gather_steps((gather_end, 3), (gather_b, 5), (gather_ab, 6))
    exchange_start(1, lambda rows: dot(r.cmixed[rows], w8(CO), 1, 1))

    def after_cross(rows, total):
        resid = r.resid_one[rows] + total
        r.resid_two[rows] = resid
        r.a3[rows] = norm(resid, 2)

    by_rows(1, after_cross)
    bring_cot.wait()

    def up_half(first):
        @pl.loop(0, half // TILE)
        def _(n):
            cols = pl.ds(pl.multiple_of(first + n * TILE, TILE), TILE)
            pre = dot(r.a3[...], wide(UP, cols), 1, 0)
            below = 0.5 * (1.0 + lax.erf(pre * ROOT_HALF))
            r.act[:, cols] = (pre * below).astype(LOW)
            slope = below + pre * (DENSITY * jnp.exp(-0.5 * (pre * pre)))
            r.slope[:, cols] = slope.astype(r.slope.dtype)

    def grad_wide(which, left, right, first):
        cols = pl.ds(first, half)
        put_wide(which, cols, dot(left[...], right[:, cols], 0, 0))

    gather_steps((gather_end, 4), (gather_b, 6), (gather_ab, 7))
    up_half(0)
    gather_steps((gather_end, 5), (gather_b, 7))
    up_half(half)
    grad_wide(DOWN, r.cot, r.act, 0)
    reduce_start(0)
    grad_wide(DOWN, r.cot, r.act, half)

    gather_steps((gather_end, 6), (gather_end, 7))
    reduce_start(1)
    everything = pl.ds(0, g.ff)
    exchange_start(2, lambda rows: dot(r.act[rows], wide(DOWN, everything), 1, 1))

    @pl.loop(0, g.ff // TILE)
    def _(n):
        cols = pl.ds(pl.multiple_of(n * TILE, TILE), TILE)
        grad_act = dot(r.cot[...], wide(DOWN, cols), 1, 0)
        r.slope[:, cols] = (grad_act * r.slope[:, cols].astype(F32)).astype(LOW)

    exchange_start(3, lambda rows: dot(r.slope[rows], wide(UP, everything), 1, 1))
    grad_wide(UP, r.a3, r.slope, 0)
    reduce_start(2)
    grad_wide(UP, r.a3, r.slope, half)
    reduce_start(3)

    def after_down(rows, total):
        r.a3[rows] = (r.resid_two[rows] + total).astype(LOW)

    by_rows(2, after_down)
    write_out = pltpu.make_async_copy(r.a3, r.out, r.write_sem.at[0])
    write_out.start()

    def after_up(rows, total):
        grad = r.cot[rows].astype(F32) + norm_back(2, r.resid_two[rows], total)
        r.grad[rows] = grad
        r.grad_low[rows] = grad.astype(LOW)

    by_rows(3, after_up)
    put8(CO, dot(r.grad_low[...], r.cmixed[...], 0, 0))
    reduce_start(4)
    r.g_mixed[...] = dot(r.grad_low[...], w8(CO), 1, 0).astype(LOW)

    @pl.loop(0, g.micro)
    def _(m):
        for h in range(pairs):
            lanes = lanes_of(h)
            queries, grads, soft = [], [], []
            for n in range(g.row_mb):
                row = m * g.row_mb + n
                rows = pl.ds(pl.multiple_of(row * g.seq, g.seq), g.seq)
                image = m * g.img_mb + r.image_ids[row]
                grads.append(stack_heads(r.g_mixed[rows, lanes], masks))
                queries.append(stack_heads(r.cq[rows, lanes], masks))
                weights_low = r.cross_p[row * pairs + h]
                soft.append(weights_low)
                prob = weights_low.astype(F32)
                grad_p = dot(r.kv[1, image, :, lanes], grads[-1], 1, 1)
                inner = jnp.sum(prob * grad_p, axis=0, keepdims=True)
                grad_s = (prob * (grad_p - inner)).astype(LOW)
                r.cross_ds[:, lanes_of(n)] = grad_s
                grad_q = join_heads(dot(grad_s, r.kv[0, image, :, lanes], 0, 0)) * score_scale
                r.g_cq[rows, lanes] = grad_q.astype(LOW)
            soft = jnp.concatenate(soft, axis=1)
            for i in range(g.img_mb):
                chosen = [
                    jnp.where(r.image_ids[m * g.row_mb + n] == i, jnp.ones((1, PAIR), F32), 0.0).astype(LOW)
                    for n in range(g.row_mb)
                ]
                picked = jnp.concatenate([q * c for q, c in zip(queries, chosen)], axis=0)
                r.kv[0, m * g.img_mb + i, :, lanes] = (dot(r.cross_ds[...], picked, 1, 0) * score_scale).astype(LOW)
                picked = jnp.concatenate([v * c for v, c in zip(grads, chosen)], axis=0)
                r.kv[1, m * g.img_mb + i, :, lanes] = dot(soft, picked, 1, 0).astype(LOW)

    exchange_start(4, lambda rows: dot(r.g_cq[rows], w8(CQ), 1, 1))
    for j in range(2):
        put8(CKV + j, dot(r.enc[...], r.kv[j].reshape(g.images * g.ctx, g.f), 0, 0))
    reduce_start(5)
    put8(CQ, dot(r.a2[...], r.g_cq[...], 0, 0))
    reduce_start(6)

    def after_query(rows, total):
        grad = r.grad[rows] + norm_back(1, r.resid_one[rows], total)
        r.grad[rows] = grad
        r.grad_low[rows] = grad.astype(LOW)

    by_rows(4, after_query)
    put8(SO, dot(r.grad_low[...], r.mixed[...], 0, 0))
    reduce_start(7)
    r.g_mixed[...] = dot(r.grad_low[...], w8(SO), 1, 0).astype(LOW)

    @pl.loop(0, g.t // PAIR)
    def _(p):
        rows = pl.ds(pl.multiple_of(p * PAIR, PAIR), PAIR)
        for h in range(pairs):
            lanes = lanes_of(h)
            queries = stack_heads(r.qkv[0, rows, lanes], masks)
            grads = stack_heads(r.g_mixed[rows, lanes], masks)
            weights_low = r.self_p[p, h]
            prob = weights_low.astype(F32)
            grad_p = dot(r.qkv[2, rows, lanes], grads, 1, 1)
            inner = jnp.sum(prob * grad_p, axis=0, keepdims=True)
            grad_s = (prob * (grad_p - inner)).astype(LOW)
            grad_q = join_heads(dot(grad_s, r.qkv[1, rows, lanes], 0, 0)) * score_scale
            grad_k = dot(grad_s, queries, 1, 0) * score_scale
            grad_v = dot(weights_low, grads, 1, 0)
            r.qkv[0, rows, lanes] = grad_q.astype(LOW)
            r.qkv[1, rows, lanes] = grad_k.astype(LOW)
            r.qkv[2, rows, lanes] = grad_v.astype(LOW)

    for j in range(3):
        put8(QKV + j, dot(r.a1[...], r.qkv[j], 0, 0))
    reduce_start(8)
    exchange_start(
        5,
        lambda rows: dot(r.qkv[0, rows], w8(QKV), 1, 1)
        + dot(r.qkv[1, rows], w8(QKV + 1), 1, 1)
        + dot(r.qkv[2, rows], w8(QKV + 2), 1, 1),
    )

    def features(j, h):
        if g.comm:
            return r.w8[j, pl.ds(h * (g.nz // 2), g.nz // 2)].reshape(g.d // 2, g.f)
        return r.w8[j, pl.ds(pl.multiple_of(h * (g.d // 2), g.d // 2), g.d // 2)]

    def encoder_part(image, h):
        return dot(r.kv[0, image], features(CKV, h), 1, 1) + dot(r.kv[1, image], features(CKV + 1, h), 1, 1)

    strips = g.d // 2 // PAIR

    def encoder_keep(image, value):
        for h in range(strips):
            r.cross_p[image * strips + h] = value[:, h * PAIR:(h + 1) * PAIR].astype(LOW)

    def encoder_copy(image):
        part = pl.ds(image * strips, strips)
        return remote(r.cross_p.at[part], r.enc_land.at[part], r.enc_s.at[image], r.enc_r.at[image], sibling)

    for image in range(g.images):
        encoder_keep(image, encoder_part(image, 1 - mp))
        encoder_copy(image).start()

    def after_qkv(rows, total):
        grad = r.grad[rows] + norm_back(0, r.hidden[rows].astype(F32), total)
        r.grad[rows] = grad

    by_rows(5, after_qkv)
    write = [write_out, pltpu.make_async_copy(r.grad, r.in_grad, r.write_sem.at[1])]
    write[1].start()

    for i in range(3):
        r.gain_total[0, i:i + 1] = jnp.sum(r.gain_sum[i], axis=0, keepdims=True)
    if g.comm:
        first = len(small)
        meet(r.gain_total.at[0], r.total_land.at[0], first, at_x).wait_recv()
        r.gain_total[1] = r.gain_total[0] + r.total_land[0]
        meet(r.gain_total.at[1], r.total_land.at[1], first + 1, at_y).wait_recv()
        r.gain_total[2] = r.gain_total[1] + r.total_land[1]
        for k in range(g.nz - 1):
            meet(r.gain_total.at[2], r.total_land.at[2 + k], first + 2 + k, at_z[k])

    reduce_start(9)
    for image in range(g.images):
        encoder_copy(image).wait_recv()
        encoder_copy(image).wait_send()
        landed = jnp.concatenate([r.enc_land[image * strips + h] for h in range(strips)], axis=1)
        encoder_keep(image, encoder_part(image, mp) + landed.astype(F32))
        rows = pl.ds(image * g.ctx, g.ctx)
        for h in range(strips):
            write.append(pltpu.make_async_copy(
                r.cross_p.at[image * strips + h], r.enc_grad.at[rows, lanes_of(h)],
                r.write_sem.at[2 + image * strips + h],
            ))
            write[-1].start()
    reduce_start(10)
    reduce_start(11)
    if g.comm:
        total = r.gain_total[2]
        for k in range(g.nz - 1):
            small[first + 2 + k].wait_recv()
            total = total + r.total_land[2 + k]
        r.gain_out[...] = total
    else:
        r.gain_out[...] = r.gain_total[0]
    for copy in write:
        copy.wait()
    for copy in small + started:
        copy.wait_send()


def run_layer(g, operands):
    vmem = pl.BlockSpec(memory_space=pltpu.VMEM)
    smem = pl.BlockSpec(memory_space=pltpu.SMEM)
    anywhere = pl.BlockSpec(memory_space=pl.ANY)
    shape = jax.ShapeDtypeStruct
    ins = dict(
        image_ids=smem, seg=vmem, hidden=vmem, gains_in=vmem, cot_in=anywhere, enc_in=anywhere,
        qkv_in=anywhere, so_in=anywhere, cq_in=anywhere, ckv_in=anywhere, co_in=anywhere,
        up_in=anywhere, down_in=anywhere,
    )
    outs = dict(
        out=(shape((g.t, g.d), LOW), anywhere),
        in_grad=(shape((g.t, g.d), F32), anywhere),
        enc_grad=(shape((g.images * g.ctx, g.d // 2), LOW), anywhere),
        gain_out=(shape((8, g.d), F32), vmem),
    )
    grid = (g.nz, 4, g.blk) if g.comm else (g.d,)
    dma = pltpu.SemaphoreType.DMA
    scratch = dict(
        w8=pltpu.VMEM((MATS, *grid, g.f), LOW),
        wf=pltpu.VMEM((2, *grid, g.ff), LOW),
        enc=pltpu.VMEM((g.images * g.ctx, g.d), LOW),
        cot=pltpu.VMEM((g.t, g.d), LOW),
        gains=pltpu.VMEM((3, 1, g.d), F32),
        gain_sum=pltpu.VMEM((3, 8, g.d), F32),
        gain_total=pltpu.VMEM((3, 8, g.d), F32),
        bias=pltpu.VMEM((g.t // PAIR, PAIR, PAIR), F32),
        a1=pltpu.VMEM((g.t, g.d), LOW),
        a2=pltpu.VMEM((g.t, g.d), LOW),
        a3=pltpu.VMEM((g.t, g.d), LOW),
        qkv=pltpu.VMEM((3, g.t, g.f), LOW),
        mixed=pltpu.VMEM((g.t, g.f), LOW),
        cq=pltpu.VMEM((g.t, g.f), LOW),
        cmixed=pltpu.VMEM((g.t, g.f), LOW),
        g_mixed=pltpu.VMEM((g.t, g.f), LOW),
        g_cq=pltpu.VMEM((g.t, g.f), LOW),
        kv=pltpu.VMEM((2, g.images, g.ctx, g.f), LOW),
        self_p=pltpu.VMEM((g.t // PAIR, g.f // PAIR, PAIR, 2 * PAIR), LOW),
        cross_p=pltpu.VMEM((g.rows * (g.f // PAIR), g.ctx, PAIR), LOW),
        cross_ds=pltpu.VMEM((g.ctx, g.row_mb * PAIR), LOW),
        resid_one=pltpu.VMEM((g.t, g.d), F32),
        resid_two=pltpu.VMEM((g.t, g.d), F32),
        grad=pltpu.VMEM((g.t, g.d), F32),
        grad_low=pltpu.VMEM((g.t, g.d), LOW),
        act=pltpu.VMEM((g.t, g.ff), LOW),
        slope=pltpu.VMEM((g.t, g.ff), LOW),
        stage=pltpu.VMEM((2, g.t, g.d), LOW),
        land=pltpu.VMEM((3, g.t, g.d), LOW),
        enc_land=pltpu.VMEM((g.images * (g.d // 2 // PAIR), g.ctx, PAIR), LOW),
        local_sem=dma((9,)),
        ex_s=dma((6, 2)), ex_r=dma((6, 2)),
        enc_s=dma((g.images,)), enc_r=dma((g.images,)),
        write_sem=dma((2 + g.images * (g.d // 2 // PAIR),)),
    )
    if g.comm:
        outs.update(
            g8_out=(shape((MATS, g.blk, g.f), F32), vmem),
            gf_out=(shape((2, g.blk, g.ff), F32), vmem),
        )
        hops = g.nz - 1
        scratch.update(
            p8=pltpu.VMEM((MATS, *grid, g.f), LOW),
            pf=pltpu.VMEM((2, *grid, g.ff), LOW),
            lb8=pltpu.VMEM((2, MATS, g.nz, 1, g.blk, g.f), LOW),
            lbf=pltpu.VMEM((2, 2, g.nz, 1, g.blk, g.ff), LOW),
            la8=pltpu.VMEM((MATS, g.nz, 1, g.blk, g.f), LOW),
            laf=pltpu.VMEM((2, g.nz, 1, g.blk, g.ff), LOW),
            lz8=pltpu.VMEM((MATS, hops, 1, g.blk, g.f), LOW),
            lzf=pltpu.VMEM((2, hops, 1, g.blk, g.ff), LOW),
            gain_land=pltpu.VMEM((hops + 2, 16, g.d), LOW),
            gain_pass=pltpu.VMEM((2, 16, g.d), LOW),
            total_land=pltpu.VMEM((hops + 2, 8, g.d), F32),
            agz_s=dma((8, hops)), agz_r=dma((8, hops)),
            aga_s=dma((8,)), aga_r=dma((8,)),
            agb_s=dma((8, 2)), agb_r=dma((8, 2)),
            rsz_s=dma((9, hops)), rsz_r=dma((9, hops)),
            rsa_s=dma((9,)), rsa_r=dma((9,)),
            rsb_s=dma((9, 2)), rsb_r=dma((9, 2)),
            small_s=dma((2 * hops + 4,)), small_r=dma((2 * hops + 4,)),
        )
    else:
        outs.update(
            p8=(shape((MATS, g.d, g.f), LOW), vmem),
            pf=(shape((2, g.d, g.ff), LOW), vmem),
        )
    g.names = (*ins, *outs, *scratch)
    return dict(zip(outs, pl.pallas_call(
        functools.partial(layer, g),
        out_shape=[o[0] for o in outs.values()],
        in_specs=list(ins.values()),
        out_specs=[o[1] for o in outs.values()],
        scratch_shapes=list(scratch.values()),
        compiler_params=pltpu.CompilerParams(
            collective_id=0, has_side_effects=True, vmem_limit_bytes=62 * 2**20
        ),
        name="layer",
    )(*operands)))


def body(
    dp, mp, hidden, encoder_tokens, segment_ids, image_index, cotangent, norm_gains, qkv_weight,
    self_out_weight, cross_query_weight, cross_kv_weight, cross_out_weight, up_weight, down_weight,
):
    micro, row_mb, seq, d = hidden.shape
    img_mb, ctx = encoder_tokens.shape[1:3]
    blk, f = self_out_weight.shape
    g = SimpleNamespace(
        micro=micro, row_mb=row_mb, seq=seq, d=d, img_mb=img_mb, ctx=ctx, blk=blk, f=f,
        ff=up_weight.shape[1], rows=micro * row_mb, t=micro * row_mb * seq, images=micro * img_mb,
        nz=dp // 4, comm=dp % 4 == 0 and blk % 16 == 0,
    )
    row = jnp.arange(g.rows) % (PAIR // seq)
    seg = (segment_ids.reshape(g.rows, seq) + 64 * row[:, None]).astype(F32).reshape(g.t // PAIR, PAIR)
    seg = jnp.pad(seg, ((0, -seg.shape[0] % 8), (0, 0)))
    me = lax.axis_index("dp")
    if g.comm:
        gains = lax.dynamic_update_slice(jnp.zeros((16, d), LOW), norm_gains, (0, me * blk))
        weights = (qkv_weight, self_out_weight, cross_query_weight, cross_kv_weight, cross_out_weight, up_weight, down_weight)
    else:
        gains = jnp.pad(lax.all_gather(norm_gains, "dp", axis=1, tiled=True), ((0, 13), (0, 0)))
        weights = [
            lax.all_gather(w, "dp", axis=w.ndim - 2, tiled=True)
            for w in (qkv_weight, self_out_weight, cross_query_weight, cross_kv_weight, cross_out_weight, up_weight, down_weight)
        ]
    weights = list(weights)
    for i in (1, 2, 4):
        weights[i] = weights[i][None]
    o = run_layer(g, (
        image_index.reshape(g.rows), seg, hidden.reshape(g.t, d), gains, cotangent.reshape(g.t, d),
        encoder_tokens.reshape(g.images * ctx, d), *weights,
    ))
    if g.comm:
        small, wide = o["g8_out"], o["gf_out"]
        gain_grad = lax.dynamic_slice(o["gain_out"], (0, me * blk), (3, blk))
    else:
        small = lax.psum_scatter(o["p8"].astype(F32), "dp", scatter_dimension=1, tiled=True)
        wide = lax.psum_scatter(o["pf"].astype(F32), "dp", scatter_dimension=1, tiled=True)
        gain_grad = lax.psum_scatter(o["gain_out"][:3], "dp", scatter_dimension=1, tiled=True)
    return (
        o["out"].reshape(hidden.shape),
        o["in_grad"].reshape(hidden.shape),
        o["enc_grad"].astype(F32).reshape(micro, img_mb, ctx, d // 2),
        gain_grad,
        small[QKV:QKV + 3],
        small[SO],
        small[CQ],
        small[CKV:CKV + 2],
        small[CO],
        wide[UP],
        wide[DOWN],
    )


def solution(mesh):
    tokens, kept = P(None, "dp", None, None), P("dp", "mp")
    three = P(None, "dp", "mp")
    return jax.shard_map(
        functools.partial(body, mesh.shape["dp"], mesh.shape["mp"]),
        mesh=mesh,
        in_specs=(
            tokens, tokens, P(None, "dp", None), P(None, "dp"), tokens, P(None, "dp"),
            three, kept, kept, three, kept, kept, kept,
        ),
        out_specs=(
            tokens, tokens, P(None, "dp", None, "mp"), P(None, "dp"),
            three, kept, kept, three, kept, kept, kept,
        ),
        check_vma=False,
    )
```

time: 1720 us -> 228 us (0.13)
  waiting for transfers between devices: 1080 us -> 0 us
  Pallas kernels: 0 us -> 209 us
  local copies, waits for them, and re-layouts: 209 us -> 16 us
  matrix products: 169 us -> 0 us
  blocking collectives: 168 us -> 0 us
  other arithmetic: 59.6 us -> 2.04 us
    reduce_scatter x4 -> x0, waiting for transfers between devices: 525 us -> none  [the longest x1 142 us: reduce_weight_grads(): lax.psum_scatter(gradients[6], 'dp', scatter_dimension=0, tiled=True)]
    unnamed x24 -> x0, waiting for transfers between devices: 392 us -> none
    pallas_call x0 -> x1, Pallas kernels: none -> 209 us  [run_layer(): pl.pallas_call(functools.partial(layer, g), out_shape=[o[0] for o in outs...]
    dot_general x68 -> x0, matrix products: 169 us -> none  [the longest x2 20.9 us: micro_step(): jnp.einsum('ri,jrce->jice', chooser, grad_rows_kv, precision=lax.Precisio...]
    all_gather x4 -> x0, blocking collectives: 168 us -> none  [the longest x1 44.4 us: fetch_weights(): lax.all_gather(cross_query_weight, 'dp', axis=0, tiled=True)]
    all_gather x4 -> x0, waiting for transfers between devices: 122 us -> none  [the longest x1 61.7 us: fetch_weights(): lax.all_gather(up_weight, 'dp', axis=0, tiled=True)]
    unnamed x306 -> x10, local copies, waits for them, and re-layouts: 68.8 us -> 3.44 us
    another operation x28 -> x0, local copies, waits for them, and re-layouts: 56.4 us -> none  [the longest x4 24.8 us: micro_step(): jnp.stack([grad_ck, grad_cv]).reshape(2, row_count, context, -1)]
  transfers between devices with their start and end apart: 19 -> 0, of which waited for: 15 -> 0; matrix products, arithmetic and copies ran while one was open for 14% -> 0% of each run, Pallas kernels for 0% -> 0%
where the time goes in v1:
time: 228 us; the launch traced here: 227 us
  Pallas kernels  209 us (92%)
  local copies, waits for them, and re-layouts  16 us (7%)
    pallas_call x1, Pallas kernels, run_layer(): pl.pallas_call(functools.partial(layer, g), out_shape=[o[0] for o in outs...  209 us

profile of v1, /device:TPU:0, one launch (start us, length us, event | category | flops | bytes accessed | tf_op | source)
XLA Modules:
  0.0 227.4 jit_solution(7979187065493670341)
XLA Ops:
  0.6 1.3 reshape.65.refs_0_
  1.9 0.8 reshape.66
  2.7 0.1 add.29
  2.8 0.1 add.30
  2.9 0.6 pad.4.refs_1_
  3.5 1.5 dynamic_update_slice.3.refs_3_
  5.0 0.0 copy-start.3
  5.0 0.6 copy-done.3
  5.6 208.7 %layer.1 = (bf16[512,768]{1,0:T(8,128)(2,1)}, f32[512,768]{1,0:T(8,128)}, bf16[2304,384]{1,0:T(8,128)(2,1)}, f32[8,768]{1,0:T(8,128)}, f32[8,48,384]{2,1,0:T(8,128)}, /*index=5*/f32[2,48,1536]{2,1,0:T(8,128)}) custom-call(s32[8]{0:T(128)} %reshape.65.refs_0_, f32[8,128]{1,0:T(8,128)} %pad.4.refs_1_, bf16[512,768]{1,0:T(8,128)(2,1)} %bitcast.23, ...), custom_call_target="tpu_custom_call" | custom-call | tf_op jit(solution)/shard_map/layer/pallas_call | solution.py:721
  214.3 0.0 copy-start
  214.3 1.5 constant_dynamic-slice_fusion
  215.8 1.6 slice.24
  217.4 1.6 slice.21
  219.0 1.6 slice_bitcast_fusion.2
  220.7 1.9 slice_bitcast_fusion
  222.6 0.0 copy-done
  222.6 0.0 copy-start.2
  222.6 2.0 convert.1
  224.6 0.0 copy-done.2
  224.6 0.0 copy-start.1
  224.6 0.9 copy.27
  225.5 0.8 copy-done.1
  226.3 1.1 copy.28
  (3 shorter events, 0.0 us)
Async XLA Ops:
  5.0 0.6 copy-start.3
  214.3 8.3 %copy-start = (bf16[2304,384]{1,0:T(8,128)(2,1)S(1)}, bf16[2304,384]{1,0:T(8,128)(2,1)}, u32[]{:S(2)}) copy-start(bf16[2304,384]{1,0:T(8,128)(2,1)} %get-tuple-element.19) | copy-start | bytes 5308420
  222.6 2.0 copy-start.2
  224.6 1.7 copy-start.1
